TPU v7x, 1024 devices: a whole 4x8x16 slice. The times are simulated.
1024 devices in a mesh: dp: 64 (over y_hi, z), fsdp: 16 (over y_lo, x, core).
Axes of the slice: x: 4, y: 8 (y_hi: 4, y_lo: 2; y = y_hi * 2 + y_lo), z: 16, core: 2. Of those that a mesh axis runs over, the one named last changes fastest.
Arguments:
- features: bfloat16 [401408, 512], P(('dp', 'fsdp')), may hold values from -6 to 6
- shortcut: bfloat16 [401408, 2048], P(('dp', 'fsdp')), may hold values from -6 to 6
- conv_weight: bfloat16 [2048, 512], P('fsdp'), may hold values from -0.25 to 0.25
- proj_weight: bfloat16 [2048, 256], P('fsdp'), may hold values from -0.125 to 0.125
- partner: int32 [8192], P(('dp', 'fsdp')), may hold values from 0 to 511, as said below
Outputs:
- grad_conv: float32 [2048, 512], P('fsdp')
- grad_proj: float32 [2048, 256], P('fsdp')
- group_loss: float32 [16], P('fsdp')
Inputs may be any that keep to these rules, and one draw needn't show every extreme that they name: Each image's partner is another image of its group, given as its member index, and the pairing is mutual: the partner of the partner is the image itself.
All inputs are finite; a program needn't handle non-finite values.
Results may differ from a plain program's by a relative error of at most 0.035.
Values may be sent and summed in bfloat16 or wider, within the bound.
A program may use at most 32 MiB of HBM per device.

v0:
```python
import jax
import jax.numpy as jnp
from jax import lax
from jax.sharding import PartitionSpec as P

POS = 49


gamma_weight = 3.0
epsilon = 1e-06


def pool_rows(hidden, images):
    return jnp.mean(hidden.reshape(images, POS, hidden.shape[-1]), axis=1)


def forward_cols(features, short_cols, conv_rows):
    preact = lax.dot_general(
        features, conv_rows, (((1,), (1,)), ((), ())), preferred_element_type=jnp.float32
    )
    return jnp.maximum(preact + short_cols.astype(jnp.float32), 0.0)


def grad_block(features, hidden_cols, proj_rows, pooled_cols, grad_embed, images):
    count = proj_rows.shape[0]
    grad_pool = (
        lax.dot_general(
            grad_embed, proj_rows, (((1,), (1,)), ((), ())), preferred_element_type=jnp.float32
        )
        / POS
    )
    spread_rows = jnp.broadcast_to(grad_pool[:, None, :], (images, POS, count)).reshape(
        images * POS, count
    )
    grad_hidden = jnp.where(hidden_cols > 0, spread_rows, 0.0).astype(jnp.bfloat16)
    conv_part = lax.dot_general(
        grad_hidden, features, (((0,), (0,)), ((), ())), preferred_element_type=jnp.float32
    )
    proj_part = lax.dot_general(
        pooled_cols, grad_embed, (((0,), (0,)), ((), ())), preferred_element_type=jnp.float32
    )
    return jnp.concatenate([conv_part, proj_part], axis=1)


def local(features, shortcut, conv_weight, proj_weight, partner):
    images = features.shape[0] // POS
    width_in = features.shape[1]
    conv_all, proj_all = (
        lax.all_gather(conv_weight, "fsdp", axis=0, tiled=True),
        lax.all_gather(proj_weight, "fsdp", axis=0, tiled=True),
    )
    hidden = forward_cols(features, shortcut, conv_all)
    pooled = pool_rows(hidden, images).astype(jnp.bfloat16)
    embed_own = jnp.dot(pooled, proj_all, preferred_element_type=jnp.float32)
    all_embed = lax.all_gather(embed_own, "dp", axis=0, tiled=True)
    count = all_embed.shape[0]
    center = jnp.mean(all_embed, axis=0)
    spread = 2.0 * jnp.mean(jnp.sum((all_embed - center) ** 2, axis=1))
    squares_all = jnp.sum(all_embed * all_embed, axis=1)
    squares_own = jnp.sum(embed_own * embed_own, axis=1)
    inner = jnp.dot(embed_own, all_embed.T, precision=lax.Precision.HIGHEST)
    kernel = jnp.exp(-(squares_own[:, None] + squares_all[None, :] - 2.0 * inner) / (2.0 * spread))
    row_own = jnp.mean(kernel, axis=1)
    onehot = (partner[:, None] == jnp.arange(count, dtype=jnp.int32)[None, :]).astype(jnp.float32)
    positive_own = jnp.sum(kernel * onehot)
    scale_sq = float(count - 1) ** 2
    row_all = lax.all_gather(row_own, "dp", axis=0, tiled=True)
    total_mean = jnp.mean(row_all)
    centered = kernel - row_own[:, None] - row_all[None, :] + total_mean
    square_sum, positive_sum = lax.psum((jnp.sum(centered * centered), positive_own), "dp")
    root = jnp.sqrt(square_sum / scale_sq + epsilon)
    loss_value = -(positive_sum / count - total_mean) + gamma_weight * root
    groups_count = lax.axis_size("fsdp")
    coeff = (
        -onehot / count + 1.0 / (count * count) + gamma_weight * centered / (scale_sq * root)
    ) / groups_count
    weighted = coeff * kernel
    grad_embed = -(2.0 / spread) * (
        jnp.sum(weighted, axis=1)[:, None] * embed_own
        - jnp.dot(weighted, all_embed, precision=lax.Precision.HIGHEST)
    )
    grad_embed = grad_embed.astype(jnp.bfloat16)
    shard_term = lax.psum_scatter(
        grad_block(features, hidden, proj_all, pooled, grad_embed, images).astype(jnp.bfloat16),
        "fsdp",
        scatter_dimension=0,
        tiled=True,
    ).astype(jnp.float32)
    total = lax.psum(shard_term, "dp")
    return (total[:, :width_in], total[:, width_in:], jnp.reshape(loss_value, (1,)))


def solution(mesh):
    return jax.shard_map(
        local,
        mesh=mesh,
        in_specs=(
            P(("dp", "fsdp"), None),
            P(("dp", "fsdp"), None),
            P("fsdp", None),
            P("fsdp", None),
            P(("dp", "fsdp")),
        ),
        out_specs=(P("fsdp", None), P("fsdp", None), P("fsdp")),
        check_vma=False,
    )
```

profile of v0, /device:TPU:6, one launch (start us, length us, event | category | flops | bytes accessed | tf_op | source)
XLA Modules:
  0.0 982.4 jit_solution(5917963417725507350)
XLA Ops:
  7.2 0.7 all-gather.3.cloned.1.call-update
  8.0 0.7 all-gather.5.cloned.1.call-update
  8.7 1.3 dynamic-slice
  10.6 52.6 %all-gather.3.cloned.1.call-done = bf16[2048,512]{1,0:T(8,128)(2,1)} async-done(((bf16[128,512]{1,0:T(8,128)(2,1)}), bf16[2048,512]{1,0:T(8,128)(2,1)}) %all-gather.3.cloned.1.call-update) | async-done | bytes 2097168 | tf_op jit(solution)/shard_map/all_gather | solution.py:49
  63.3 5.8 broadcast_maximum_fusion
  69.1 4.1 reshape.27
  73.2 2.5 reduce_sum.94
  75.7 33.5 %all-gather.5.cloned.1.call-done = bf16[2048,256]{1,0:T(8,128)(2,1)} async-done(((bf16[128,256]{1,0:T(8,128)(2,1)}), bf16[2048,256]{1,0:T(8,128)(2,1)}) %all-gather.5.cloned.1.call-update) | async-done | bytes 1048592 | tf_op jit(solution)/shard_map/all_gather | solution.py:50
  109.1 1.7 multiply_reduce_fusion.3
  110.8 159.8 %all_gather.14 = f32[512,256]{1,0:T(8,128)S(1)} all-gather(f32[8,256]{1,0:T(8,128)S(1)} %get-tuple-element.23), channel_id=1, replica_groups=mesh['dp'=64,'fsdp'=16] {'dp'}, dimensions={0}, use_global_device_ids=true | all-gather | bytes 532480 | tf_op jit(solution)/shard_map/all_gather | solution.py:55
  270.6 0.1 reduce_sum.95
  270.7 0.8 multiply_reduce_fusion
  272.1 0.6 fusion.13
  272.8 0.1 broadcast_multiply_fusion.1
  272.9 152.4 %all-reduce = f32[512]{0:T(512)S(1)} all-reduce(f32[512]{0:T(512)S(1)} %get-tuple-element.19), channel_id=1, replica_groups=mesh['dp'=64,'fsdp'=16] {'dp'}, use_global_device_ids=true, to_apply=%add | all-reduce | flops 512 | bytes 4096
  425.3 0.6 reduce_sum.100
  426.5 0.7 multiply_reduce_fusion.2
  427.2 155.0 %psum.21 = f32[]{:T(128)} all-reduce(f32[]{:T(128)} %multiply_reduce_fusion.2), channel_id=1, replica_groups=mesh['dp'=64,'fsdp'=16] {'dp'}, use_global_device_ids=true, to_apply=%region_8.0 | all-reduce | flops 1 | bytes 8 | tf_op jit(solution)/shard_map/psum | solution.py:70
  583.6 0.7 select_reduce_fusion
  584.4 0.4 fusion.6
  584.7 1.5 convolution_convert_fusion.1
  586.2 0.4 convolution_multiply_fusion
  586.6 0.2 broadcast_in_dim.3
  586.8 1.7 reshape.28
  588.5 3.8 convolution_convert_fusion
  592.3 0.2 pad_maximum_fusion
  592.5 2.8 copy.14
  595.4 59.5 %reduce-scatter.4.cloned.1.call-done = bf16[128,768]{1,0:T(8,128)(2,1)} async-done(((bf16[2048,768]{1,0:T(8,128)(2,1)}), bf16[128,768]{1,0:T(8,128)(2,1)}) %reduce-scatter.4.cloned.1.call-update) | async-done | bytes 196624
  654.8 1.1 copy.15
  655.9 316.5 %all-reduce.3 = (f32[128,768]{0,1:T(8,128)S(1)}, f32[]{:T(128)}) all-reduce(bf16[128,768]{0,1:T(8,128)(2,1)S(1)} %copy.15, f32[]{:T(128)} %get-tuple-element.14), channel_id=1, replica_groups=mesh['dp'=64,'fsdp'=16] {'dp'}, use_global_device_ids=true, to_apply=%region_11.0 | all-reduce | flops 98305 | bytes 589832 | tf_op jit(solution)/shard_map/psum | solution.py:89
  973.2 0.8 copy.12
  974.0 0.8 copy.13
  (16 shorter events, 0.2 us)
Async XLA Ops:
  7.2 56.1 %copy-start = (bf16[392,512]{1,0:T(8,128)(2,1)S(1)}, bf16[392,512]{1,0:T(8,128)(2,1)}, u32[]{:S(2)}) copy-start(bf16[392,512]{1,0:T(8,128)(2,1)} %param.5) | copy-start | bytes 1204228
  7.2 56.1 %all-gather.3.cloned.1.call-start = ((), (), s32[]{:S(2)}) async-start(), calls=%async_computation.1 | async-start | bytes 2228224 | tf_op jit(solution)/shard_map/all_gather | solution.py:49
  7.9 101.2 %all-gather.5.cloned.1.call-start = ((), (), s32[]{:S(2)}) async-start(), calls=%async_computation.2 | async-start | bytes 1114112 | tf_op jit(solution)/shard_map/all_gather | solution.py:50
  8.7 646.2 %reduce-scatter.4.cloned.1.call-start = ((), (), s32[]{:S(2)}) async-start(), calls=%async_computation.3 | async-start | bytes 3342336
  73.2 510.5 %copy-start.3 = (s32[8]{0:T(128)S(1)}, s32[8]{0:T(128)}, u32[]{:S(2)}) copy-start(s32[8]{0:T(128)} %param.9) | copy-start | bytes 100
  109.1 477.0 %copy-start.1 = (bf16[2048,256]{1,0:T(8,128)(2,1)S(1)}, bf16[2048,256]{1,0:T(8,128)(2,1)}, u32[]{:S(2)}) copy-start(bf16[2048,256]{1,0:T(8,128)(2,1)} %all-gather.5.cloned.1.call-done) | copy-start | bytes 3145732
  588.5 3.8 copy-start.2
Sparse Core Ops, SparseCore 0:
  10.7 52.4 all-gather.2
  66.0 43.0 all-gather.4
  595.5 59.3 reduce-scatter.3
where the time goes:
time: 985 us; the launch traced here: 982 us
  blocking collectives  784 us (80%)
  waiting for transfers between devices  147 us (15%)
  between operations  19 us (2%)
  matrix products  14.1 us (1%)
  local copies, waits for them, and re-layouts  12.9 us (1%)
    psum x1, blocking collectives, local(): total = lax.psum(shard_term, 'dp')  317 us
    all_gather x1, blocking collectives, local(): all_embed = lax.all_gather(embed_own, 'dp', axis=0, tiled=True)  160 us
    psum x1, blocking collectives, local(): lax.psum((jnp.sum(centered * centered), positive_own), 'dp')  155 us
    unnamed x1, blocking collectives  152 us
    unnamed x4, waiting for transfers between devices  60.9 us
    all_gather x1, waiting for transfers between devices, local(): lax.all_gather(conv_weight, 'fsdp', axis=0, tiled=True)  52.6 us
    all_gather x1, waiting for transfers between devices, local(): lax.all_gather(proj_weight, 'fsdp', axis=0, tiled=True)  33.5 us
  transfers between devices with their start and end apart: 3, of which 3 were waited for; matrix products, arithmetic and copies ran while one was open for 1% of the time, Pallas kernels for 0%

commit v1 on v0

v1 whole, which is shorter than its diff:
```python
import jax
import jax.numpy as jnp
from jax import lax
from jax.experimental import pallas as pl
from jax.experimental.pallas import tpu as pltpu
from jax.sharding import PartitionSpec as P

MESH = pl.DeviceIdType.MESH
HIGH = lax.Precision.HIGHEST
BF16 = jnp.bfloat16
F32 = jnp.float32

POS = 49
GAMMA = 3.0
EPSILON = 1e-06

YH, ZH, ZL = 4, 4, 4
YL, X = 2, 4


def dot(a, b, dims=((1,), (0,)), precision=None):
    return lax.dot_general(
        a, b, (dims, ((), ())), precision=precision, preferred_element_type=F32
    )


def kernel(
    feat_h, short_h, conv_h, proj_h, partner_s,
    oconv, oproj, oloss,
    feat, short, featT, W, PW, hid, pooled, part, emb, zbuf, kmat, rcol,
    term, core_in, pair_sum, group_in,
    red0, red0_in, red1, red1_in, red2, fin,
    lsem, ssem, rsem,
):
    chips = YL * X
    dp = YH * ZH * ZL
    images = 8
    width = feat.shape[1]
    emb_w = emb.shape[2]
    group = dp * images

    d = lax.axis_index("dp")
    f = lax.axis_index("fsdp")
    yh = lax.div(d, ZH * ZL)
    zh = lax.rem(lax.div(d, ZL), ZH)
    zl = lax.rem(d, ZL)
    chip = lax.div(f, 2)
    yl = lax.div(chip, X)
    x = lax.rem(chip, X)
    c = lax.rem(f, 2)

    def dev_chip(ch, core):
        return (d, ch * 2 + core)

    def dev_dp(a, b, e):
        return ((a * ZH + b) * ZL + e, f)

    used = [0]
    pending = []

    def send(src, dst, dev):
        i = used[0]
        used[0] += 1
        copy = pltpu.make_async_remote_copy(
            src_ref=src, dst_ref=dst, send_sem=ssem.at[i], recv_sem=rsem.at[i],
            device_id=dev, device_id_type=MESH,
        )
        copy.start()
        pending.append(copy)
        return copy

    offsets = [(dy, dx) for dy in range(YL) for dx in range(X)]
    offsets.sort(key=lambda o: (o[0] + min(o[1], X - o[1]), o[0]))

    def to_chip(o):
        return lax.rem(yl + o[0], YL) * X + lax.rem(x + o[1], X)

    def from_chip(o):
        return lax.rem(yl + YL - o[0], YL) * X + lax.rem(x + X - o[1], X)

    mine = pl.ds(pl.multiple_of(c * 128, 128), 128)
    local = [
        pltpu.make_async_copy(conv_h, W.at[chip, mine], lsem.at[0]),
        pltpu.make_async_copy(feat_h, feat, lsem.at[1]),
        pltpu.make_async_copy(short_h, short, lsem.at[2]),
        pltpu.make_async_copy(proj_h, PW.at[chip, mine], lsem.at[3]),
    ]
    for copy in local:
        copy.start()

    peers = [dev_chip(chip, 1 - c)]
    peers += [dev_chip(to_chip(o), c) for o in offsets[1:]]
    peers += [dev_dp(lax.rem(yh + j, YH), zh, zl) for j in range(1, YH)]
    peers += [dev_dp(yh, lax.rem(zh + j, ZH), zl) for j in range(1, ZH)]
    peers += [dev_dp(yh, zh, lax.rem(zl + j, ZL)) for j in range(1, ZL)]
    barrier = pltpu.get_barrier_semaphore()
    for peer in peers:
        pl.semaphore_signal(barrier, inc=1, device_id=peer, device_id_type=MESH)

    slot = (zl * YH + yh) * ZH + zh
    row8 = lax.broadcasted_iota(jnp.int32, (images, 128), 0)
    column = jnp.zeros((images, 128), jnp.int32)
    for i in range(images):
        column = jnp.where(row8 == i, partner_s[i], column)
    part[pl.ds(slot, 1)] = column.astype(F32)[None]

    pl.semaphore_wait(barrier, len(peers))

    other = dev_chip(chip, 1 - c)
    conv_direct = {}
    for o in offsets[1:]:
        conv_direct[o] = send(conv_h, W.at[chip, mine], dev_chip(to_chip(o), c))
    conv_pair = {offsets[0]: send(conv_h, W.at[chip, mine], other)}

    def dp_stage(buf, stage):
        if stage == 0:
            base, size, n = slot, 1, ZH
            dev = lambda j: dev_dp(yh, lax.rem(zh + j, ZH), zl)
        elif stage == 1:
            base, size, n = (zl * YH + yh) * ZH, ZH, YH
            dev = lambda j: dev_dp(lax.rem(yh + j, YH), zh, zl)
        else:
            base, size, n = zl * YH * ZH, YH * ZH, ZL
            dev = lambda j: dev_dp(yh, zh, lax.rem(zl + j, ZL))
        view = buf.at[pl.ds(base, size)]
        return [send(view, view, dev(j)) for j in range(1, n)]

    def arrive(copies):
        for copy in copies:
            copy.wait_recv()

    part_copies = dp_stage(part, 0)
    proj_direct = {}
    for o in offsets[1:]:
        proj_direct[o] = send(proj_h, PW.at[chip, mine], dev_chip(to_chip(o), c))
    proj_pair = {offsets[0]: send(proj_h, PW.at[chip, mine], other)}

    ri = lax.broadcasted_iota(jnp.int32, (images, images * POS), 1)
    ii = lax.broadcasted_iota(jnp.int32, (images, images * POS), 0)
    pool_mat = jnp.where((ri >= ii * POS) & (ri < ii * POS + POS), 1.0, 0.0).astype(BF16)
    ri = lax.broadcasted_iota(jnp.int32, (images * POS, images), 0)
    ii = lax.broadcasted_iota(jnp.int32, (images * POS, images), 1)
    spread_mat = jnp.where((ri >= ii * POS) & (ri < ii * POS + POS), 1.0, 0.0).astype(BF16)

    def lanes(kk):
        return pl.ds(pl.multiple_of(kk * 256, 256), 256)

    def forward(kk):
        pre = dot(feat[...], W[kk], ((1,), (1,))) + short[:, lanes(kk)].astype(F32)
        h = jnp.maximum(pre, 0.0)
        hi = h.astype(BF16)
        low = (h - hi.astype(F32)).astype(BF16)
        hid[kk] = hi
        total = dot(pool_mat, hi) + dot(pool_mat, low)
        pooled[kk] = (total / POS).astype(BF16)

    for copy in local[:3]:
        copy.wait()
    for n, o in enumerate(offsets):
        if n:
            src = from_chip(o)
            conv_direct[o].wait_recv()
            view = W.at[src, mine]
            conv_pair[o] = send(view, view, other)
            last = offsets[n - 1]
            conv_pair[last].wait_recv()
            forward(from_chip(last))
        if n == min(1, chips - 1):
            featT[...] = jnp.transpose(feat[...].astype(F32)).astype(BF16)
    arrive(part_copies)
    part_copies = dp_stage(part, 1)
    for n, o in enumerate(offsets[1:]):
        src = from_chip(o)
        proj_direct[o].wait_recv()
        view = PW.at[src, mine]
        proj_pair[o] = send(view, view, other)
    conv_pair[offsets[-1]].wait_recv()
    forward(from_chip(offsets[-1]))
    local[3].wait()
    arrive(part_copies)
    part_copies = dp_stage(part, 2)

    own = jnp.zeros((images, emb_w), F32)
    for o in offsets:
        proj_pair[o].wait_recv()
        kk = from_chip(o)
        own = own + dot(pooled[kk], PW[kk])

    emb[pl.ds(slot, 1)] = own[None]
    for stage in range(3):
        arrive(dp_stage(emb, stage))
    arrive(part_copies)

    zall = emb[...].reshape(group, emb_w)
    center = jnp.mean(zall, axis=0, keepdims=True)
    zc = zall - center
    zbuf[...] = zc
    square = zc * zc
    spread = 2.0 * jnp.sum(square) / group
    sq_row = dot(jnp.ones((8, emb_w), F32), square, ((1,), (1,)), HIGH)[0:1]
    lane = lax.broadcasted_iota(jnp.int32, (1, group), 1)
    ls = lane // images
    lzl = ls // (YH * ZH)
    lyh = (ls // ZH) % YH
    lzh = ls % ZH
    member = (((lyh * ZH + lzh) * ZL + lzl) * images + lane % images).astype(F32)

    step = 64 if group % 64 == 0 else group
    scale = 1.0 / (2.0 * spread)

    def kernel_rows(i, carry):
        col_sum, positive = carry
        rows = pl.ds(pl.multiple_of(i * (step // images), step // images), step // images)
        at = pl.ds(pl.multiple_of(i * step, step), step)
        z = zbuf[at, :]
        inner = dot(z, zbuf[...], ((1,), (1,)), HIGH)
        sq = jnp.sum(z * z, axis=1, keepdims=True)
        kk = jnp.exp(-(sq + sq_row - 2.0 * inner) * scale)
        kmat[at, :] = kk
        rcol[at, :] = jnp.broadcast_to(jnp.mean(kk, axis=1, keepdims=True), (step, 128))
        who = part[rows].reshape(step, 128)[:, 0:1]
        positive = positive + jnp.sum(jnp.where(who == member, kk, 0.0), axis=0, keepdims=True)
        return col_sum + jnp.sum(kk, axis=0, keepdims=True), positive

    zero = jnp.zeros((1, group), F32)
    col_sum, positive = lax.fori_loop(0, group // step, kernel_rows, (zero, zero))
    row_mean = col_sum / group
    t = jnp.sum(row_mean) / group

    def square_rows(i, carry):
        at = pl.ds(pl.multiple_of(i * step, step), step)
        cen = kmat[at, :] - rcol[at, 0:1] - row_mean + t
        return carry + jnp.sum(cen * cen, axis=0, keepdims=True)

    sums = lax.fori_loop(0, group // step, square_rows, zero)
    scale_sq = float(group - 1) ** 2
    root_v = jnp.sqrt(jnp.broadcast_to(jnp.sum(sums) / scale_sq + EPSILON, (1, 128)))
    loss = -(jnp.sum(positive) / group - t) + GAMMA * root_v
    oloss[...] = loss
    root = root_v[0:1, 0:1]

    at = pl.ds(pl.multiple_of(slot * images, images), images)
    k_own = kmat[at, :]
    cen = k_own - rcol[at, 0:1] - row_mean + t
    who = part[pl.ds(slot, 1)].reshape(images, 128)[:, 0:1]
    hot = jnp.where(who == member, 1.0, 0.0)
    coeff = (-hot / group + 1.0 / (group * group) + GAMMA * cen / (scale_sq * root)) / (chips * 2)
    weighted = coeff * k_own
    z_own = zbuf[at, :]
    grad = -(2.0 / spread) * (
        jnp.sum(weighted, axis=1, keepdims=True) * z_own
        - dot(weighted, zbuf[...], precision=HIGH)
    )
    ge = grad.astype(BF16)
    geT = jnp.transpose(ge.astype(F32)).astype(BF16)

    def backward(n, kk):
        gp = (dot(ge, PW[kk], ((1,), (1,))) / POS).astype(BF16)
        rows = dot(spread_mat, gp)
        gh = jnp.where(hid[kk].astype(F32) > 0.0, rows, 0.0).astype(BF16)
        conv_t = dot(featT[...], gh).astype(BF16)
        proj_t = dot(geT, pooled[kk]).astype(BF16)
        for half in range(2):
            cols = slice(half * 128, half * 128 + 128)
            term[n, half, 0:width] = conv_t[:, cols]
            term[n, half, width:] = proj_t[:, cols]

    order = list(reversed(offsets))
    core_copies = {}
    group_copies = []

    def pair(n):
        core_copies[n].wait_recv()
        total = term[n, pl.ds(c, 1)][0].astype(F32) + core_in[n].astype(F32)
        pair_sum[n] = total.astype(BF16)
        if n < len(order) - 1:
            group_copies.append(
                send(pair_sum.at[n], group_in.at[n], dev_chip(to_chip(order[n]), c))
            )

    for n, o in enumerate(order):
        backward(n, to_chip(o))
        core_copies[n] = send(term.at[n, 1 - c], core_in.at[n], other)
        if n:
            pair(n - 1)
    last = len(order) - 1
    pair(last)
    arrive(group_copies)
    total = pair_sum[last].astype(F32)
    for n in range(last):
        total = total + group_in[n].astype(F32)
    red0[...] = total.astype(BF16).reshape(red0.shape)

    copies = []
    for j in range(1, ZL):
        q = lax.rem(zl + j, ZL)
        copies.append(send(red0.at[q], red0_in.at[j], dev_dp(yh, zh, q)))
    arrive(copies)
    total = red0[zl].astype(F32)
    for j in range(1, ZL):
        total = total + red0_in[j].astype(F32)
    red1[...] = total.astype(BF16)
    copies = []
    for j in range(1, ZH):
        q = lax.rem(zh + j, ZH)
        copies.append(send(red1.at[q], red1_in.at[j], dev_dp(yh, q, zl)))
    arrive(copies)
    total = red1[zh].astype(F32)
    for j in range(1, ZH):
        total = total + red1_in[j].astype(F32)
    red2[yh] = total.astype(BF16)
    copies = []
    for j in range(1, YH):
        q = lax.rem(yh + j, YH)
        copies.append(send(red2.at[yh], red2.at[yh], dev_dp(q, zh, zl)))
    arrive(copies)
    total = red2[0].astype(F32)
    for j in range(1, YH):
        total = total + red2[j].astype(F32)
    fin[zl, zh] = total.astype(BF16)
    copies = []
    for j in range(1, ZH):
        q = lax.rem(zh + j, ZH)
        copies.append(send(fin.at[zl, zh], fin.at[zl, zh], dev_dp(yh, q, zl)))
    arrive(copies)
    copies = []
    for j in range(1, ZL):
        q = lax.rem(zl + j, ZL)
        copies.append(send(fin.at[zl], fin.at[zl], dev_dp(yh, zh, q)))
    arrive(copies)

    result = fin[...].astype(F32).reshape(width + emb_w, 128)
    oconv[...] = jnp.transpose(result[0:width])
    oproj[...] = jnp.transpose(result[width:])

    for copy in pending:
        copy.wait_send()


def local(features, shortcut, conv_weight, proj_weight, partner):
    rows, width = features.shape
    emb_w = proj_weight.shape[1]
    chips = YL * X
    dp = YH * ZH * ZL
    group = dp * 8
    both = width + emb_w
    piece = both // (ZL * ZH)
    sends = 2 * (chips - 1 + chips) + 2 * (YH + ZH + ZL - 3) + 2 * chips - 1
    sends += 2 * (ZL - 1 + ZH - 1) + YH - 1
    hbm = pl.BlockSpec(memory_space=pl.ANY)
    vmem = pl.BlockSpec(memory_space=pltpu.VMEM)
    grad_conv, grad_proj, loss = pl.pallas_call(
        kernel,
        out_shape=(
            jax.ShapeDtypeStruct((128, width), F32),
            jax.ShapeDtypeStruct((128, emb_w), F32),
            jax.ShapeDtypeStruct((1, 128), F32),
        ),
        in_specs=[hbm, hbm, hbm, hbm, pl.BlockSpec(memory_space=pltpu.SMEM)],
        out_specs=(vmem, vmem, vmem),
        scratch_shapes=[
            pltpu.VMEM((rows, width), BF16),
            pltpu.VMEM((rows, chips * 256), BF16),
            pltpu.VMEM((width, rows), BF16),
            pltpu.VMEM((chips, 256, width), BF16),
            pltpu.VMEM((chips, 256, emb_w), BF16),
            pltpu.VMEM((chips, rows, 256), BF16),
            pltpu.VMEM((chips, 8, 256), BF16),
            pltpu.VMEM((dp, 8, 128), F32),
            pltpu.VMEM((dp, 8, emb_w), F32),
            pltpu.VMEM((group, emb_w), F32),
            pltpu.VMEM((group, group), F32),
            pltpu.VMEM((group, 128), F32),
            pltpu.VMEM((chips, 2, both, 128), BF16),
            pltpu.VMEM((chips, both, 128), BF16),
            pltpu.VMEM((chips, both, 128), BF16),
            pltpu.VMEM((chips, both, 128), BF16),
            pltpu.VMEM((ZL, ZH, piece, 128), BF16),
            pltpu.VMEM((ZL, ZH, piece, 128), BF16),
            pltpu.VMEM((ZH, piece, 128), BF16),
            pltpu.VMEM((ZH, piece, 128), BF16),
            pltpu.VMEM((YH, piece, 128), BF16),
            pltpu.VMEM((ZL, ZH, piece, 128), BF16),
            pltpu.SemaphoreType.DMA((4,)),
            pltpu.SemaphoreType.DMA((sends,)),
            pltpu.SemaphoreType.DMA((sends,)),
        ],
        compiler_params=pltpu.CompilerParams(
            collective_id=0, has_side_effects=True, vmem_limit_bytes=48 << 20
        ),
    )(features, shortcut, conv_weight, proj_weight, partner)
    return grad_conv, grad_proj, loss[0, 0:1]


def solution(mesh):
    return jax.shard_map(
        local,
        mesh=mesh,
        in_specs=(
            P(("dp", "fsdp"), None),
            P(("dp", "fsdp"), None),
            P("fsdp", None),
            P("fsdp", None),
            P(("dp", "fsdp")),
        ),
        out_specs=(P("fsdp", None), P("fsdp", None), P("fsdp")),
        check_vma=False,
    )
```

time: 985 us -> 143 us (0.15)
  blocking collectives: 784 us -> 0 us
  waiting for transfers between devices: 147 us -> 0 us
  Pallas kernels: 0 us -> 132 us
  between operations: 19 us -> 1.82 us
  matrix products: 14.1 us -> 0 us
    psum x2 -> x0, blocking collectives: 472 us -> none  [the longest x1 317 us: local(): total = lax.psum(shard_term, 'dp')]
    all_gather x1 -> x0, blocking collectives: 160 us -> none  [local(): all_embed = lax.all_gather(embed_own, 'dp', axis=0, tiled=True)]
    unnamed x1 -> x0, blocking collectives: 152 us -> none
    pallas_call x0 -> x1, Pallas kernels: none -> 132 us  [local(): pl.pallas_call(kernel, out_shape=(jax.ShapeDtypeStruct((128, width), F32)...]
    all_gather x2 -> x0, waiting for transfers between devices: 86.1 us -> none  [the longest x1 52.6 us: local(): lax.all_gather(conv_weight, 'fsdp', axis=0, tiled=True)]
    unnamed x4 -> x0, waiting for transfers between devices: 60.9 us -> none
    dot_general x7 -> x0, matrix products: 14.1 us -> none  [the longest x1 5.78 us: forward_cols(): lax.dot_general(features, conv_rows, (((1,), (1,)), ((), ())), preferred_...]
  transfers between devices with their start and end apart: 3 -> 0, of which waited for: 3 -> 0; matrix products, arithmetic and copies ran while one was open for 1% -> 0% of each run, Pallas kernels for 0% -> 0%
where the time goes in v1:
time: 143 us; the launch traced here: 140 us
  Pallas kernels  132 us (92%)
  local copies, waits for them, and re-layouts  6.17 us (4%)
  between operations  1.82 us (1%)
    pallas_call x1, Pallas kernels, local(): pl.pallas_call(kernel, out_shape=(jax.ShapeDtypeStruct((128, width), F32)...  132 us
    unnamed x12, local copies, waits for them, and re-layouts  6.17 us

profile of v1, /device:TPU:6, one launch (start us, length us, event | category | flops | bytes accessed | tf_op | source)
XLA Modules:
  0.0 140.2 jit_solution(2949270739343652774)
XLA Ops:
  0.6 0.0 copy-start
  0.6 1.4 %copy-done = bf16[392,2048]{1,0:T(8,128)(2,1)S(1)} copy-done((bf16[392,2048]{1,0:T(8,128)(2,1)S(1)}, bf16[392,2048]{1,0:T(8,128)(2,1)}, u32[]{:S(2)}) %copy-start) | copy-done | bytes 1605656
  2.1 0.0 copy-start.1
  2.1 1.0 copy-done.1
  3.0 0.0 copy-start.2
  3.1 0.9 copy-done.2
  4.0 0.0 copy-start.3
  4.0 0.8 copy-done.3
  4.8 0.0 copy-start.4
  4.8 0.7 copy-done.4
  5.5 132.2 %shard_map.76 = (f32[128,512]{1,0:T(8,128)S(1)}, f32[128,256]{1,0:T(8,128)S(1)}, f32[1,128]{1,0:T(1,128)S(1)}) custom-call(bf16[392,512]{1,0:T(8,128)(2,1)S(1)} %copy-done.1, bf16[392,2048]{1,0:T(8,128)(2,1)S(1)} %copy-done, bf16[128,512]{1,0:T(8,128)(2,1)S(1)} %copy-done.2, bf16[128,256]{1,0:T(8,128)(2,1)S(1)} %copy-done.3, s32[8]{0:T(128)S(1)} %copy-done.4), custom_call_target="tpu_custom_call" | custom-call | tf_op jit(solution)/shard_map/pallas_call | solution.py:352
  137.7 0.7 copy.11
  138.4 0.7 copy.12
Async XLA Ops:
  0.6 1.4 %copy-start = (bf16[392,2048]{1,0:T(8,128)(2,1)S(1)}, bf16[392,2048]{1,0:T(8,128)(2,1)}, u32[]{:S(2)}) copy-start(bf16[392,2048]{1,0:T(8,128)(2,1)} %short_h.1) | copy-start | bytes 4816900
  2.1 1.0 copy-start.1
  3.0 0.9 copy-start.2
  4.0 0.8 copy-start.3
  4.8 0.7 copy-start.4

commit v2 on v1

--- a/solution.py
+++ b/solution.py
@@ -6,7 +6,6 @@
 from jax.sharding import PartitionSpec as P
 
 MESH = pl.DeviceIdType.MESH
-HIGH = lax.Precision.HIGHEST
 BF16 = jnp.bfloat16
 F32 = jnp.float32
 
@@ -16,6 +15,22 @@
 
 YH, ZH, ZL = 4, 4, 4
 YL, X = 2, 4
+
+
+def far(o):
+    return o[0] > 0 and o[1] > 0
+
+
+def first_hop(o):
+    return (o[0], 0) if o[1] in (1, X - 1) else (0, o[1])
+
+
+def second_hop(o):
+    return (0, o[1]) if o[1] in (1, X - 1) else (o[0], 0)
+
+
+def near(n):
+    return [j if j <= n // 2 else j - n for j in sorted(range(1, n), key=lambda j: min(j, n - j))]
 
 
 def dot(a, b, dims=((1,), (0,)), precision=None):
@@ -27,7 +42,7 @@
 def kernel(
     feat_h, short_h, conv_h, proj_h, partner_s,
     oconv, oproj, oloss,
-    feat, short, featT, W, PW, hid, pooled, part, emb, zbuf, kmat, rcol,
+    feat, short, featT, W, PW, hid, pooled, part, emb, zbuf, parts, sqs, kmat, rcol,
     term, core_in, pair_sum, group_in,
     red0, red0_in, red1, red1_in, red2, fin,
     lsem, ssem, rsem,
@@ -70,7 +85,7 @@
         return copy
 
     offsets = [(dy, dx) for dy in range(YL) for dx in range(X)]
-    offsets.sort(key=lambda o: (o[0] + min(o[1], X - o[1]), o[0]))
+    offsets.sort(key=lambda o: (far(o), o[0] + min(o[1], X - o[1]), -o[0]))
 
     def to_chip(o):
         return lax.rem(yl + o[0], YL) * X + lax.rem(x + o[1], X)
@@ -89,10 +104,18 @@
         copy.start()
 
     peers = [dev_chip(chip, 1 - c)]
-    peers += [dev_chip(to_chip(o), c) for o in offsets[1:]]
+    peers += [dev_chip(to_chip(o), c) for o in offsets[1:] if not far(o)]
     peers += [dev_dp(lax.rem(yh + j, YH), zh, zl) for j in range(1, YH)]
     peers += [dev_dp(yh, lax.rem(zh + j, ZH), zl) for j in range(1, ZH)]
-    peers += [dev_dp(yh, zh, lax.rem(zl + j, ZL)) for j in range(1, ZL)]
+    z = zh * ZL + zl
+
+    def dev_z(j):
+        q = lax.rem(z + j + ZH * ZL, ZH * ZL)
+        return (yh * ZH * ZL + q, f)
+
+    near_z = near(ZL)
+    for j in near_z:
+        peers.append(dev_z(j))
     barrier = pltpu.get_barrier_semaphore()
     for peer in peers:
         pl.semaphore_signal(barrier, inc=1, device_id=peer, device_id_type=MESH)
@@ -107,33 +130,48 @@
     pl.semaphore_wait(barrier, len(peers))
 
     other = dev_chip(chip, 1 - c)
-    conv_direct = {}
-    for o in offsets[1:]:
-        conv_direct[o] = send(conv_h, W.at[chip, mine], dev_chip(to_chip(o), c))
-    conv_pair = {offsets[0]: send(conv_h, W.at[chip, mine], other)}
-
-    def dp_stage(buf, stage):
-        if stage == 0:
-            base, size, n = slot, 1, ZH
-            dev = lambda j: dev_dp(yh, lax.rem(zh + j, ZH), zl)
-        elif stage == 1:
-            base, size, n = (zl * YH + yh) * ZH, ZH, YH
-            dev = lambda j: dev_dp(lax.rem(yh + j, YH), zh, zl)
-        else:
-            base, size, n = zl * YH * ZH, YH * ZH, ZL
-            dev = lambda j: dev_dp(yh, zh, lax.rem(zl + j, ZL))
-        view = buf.at[pl.ds(base, size)]
-        return [send(view, view, dev(j)) for j in range(1, n)]
+
+    def block(ref, ch):
+        return ref.at[ch, mine]
+
+    def start_gather(source, ref):
+        direct = {}
+        for o in offsets[1:]:
+            if not far(o):
+                direct[o] = send(source, block(ref, chip), dev_chip(to_chip(o), c))
+        return direct, {offsets[0]: send(source, block(ref, chip), other)}
+
+    def landed(ref, o, direct, paired):
+        direct[o].wait_recv()
+        view = block(ref, from_chip(o))
+        for p in offsets:
+            if far(p) and first_hop(p) == o:
+                direct[p] = send(view, view, dev_chip(to_chip(second_hop(p)), c))
+        paired[o] = send(view, view, other)
+
+    conv_direct, conv_pair = start_gather(conv_h, W)
 
     def arrive(copies):
         for copy in copies:
             copy.wait_recv()
 
-    part_copies = dp_stage(part, 0)
-    proj_direct = {}
-    for o in offsets[1:]:
-        proj_direct[o] = send(proj_h, PW.at[chip, mine], dev_chip(to_chip(o), c))
-    proj_pair = {offsets[0]: send(proj_h, PW.at[chip, mine], other)}
+    def far_stage(buf):
+        view = buf.at[pl.ds(slot, 1)]
+        return [send(view, view, dev_dp(yh, lax.rem(zh + j, ZH), zl)) for j in range(1, ZH)]
+
+    def row(buf, y):
+        return buf.at[pl.ds((zl * YH + y) * ZH, ZH)]
+
+    def y_stage(buf):
+        view = row(buf, yh)
+        return {
+            j: send(view, view, dev_dp(lax.rem(yh + j + YH, YH), zh, zl)) for j in near(YH)
+        }
+
+    def near_stage(view):
+        return [send(view, view, dev_z(j)) for j in near_z]
+
+    part_copies = far_stage(part)
 
     ri = lax.broadcasted_iota(jnp.int32, (images, images * POS), 1)
     ii = lax.broadcasted_iota(jnp.int32, (images, images * POS), 0)
@@ -156,29 +194,28 @@
 
     for copy in local[:3]:
         copy.wait()
+    proj_direct = proj_pair = None
     for n, o in enumerate(offsets):
         if n:
-            src = from_chip(o)
-            conv_direct[o].wait_recv()
-            view = W.at[src, mine]
-            conv_pair[o] = send(view, view, other)
+            landed(W, o, conv_direct, conv_pair)
+            if n == 1:
+                proj_direct, proj_pair = start_gather(proj_h, PW)
             last = offsets[n - 1]
             conv_pair[last].wait_recv()
             forward(from_chip(last))
         if n == min(1, chips - 1):
             featT[...] = jnp.transpose(feat[...].astype(F32)).astype(BF16)
+    if chips == 1:
+        proj_direct, proj_pair = start_gather(proj_h, PW)
     arrive(part_copies)
-    part_copies = dp_stage(part, 1)
-    for n, o in enumerate(offsets[1:]):
-        src = from_chip(o)
-        proj_direct[o].wait_recv()
-        view = PW.at[src, mine]
-        proj_pair[o] = send(view, view, other)
+    part_copies = y_stage(part)
+    for o in offsets[1:]:
+        landed(PW, o, proj_direct, proj_pair)
     conv_pair[offsets[-1]].wait_recv()
     forward(from_chip(offsets[-1]))
     local[3].wait()
-    arrive(part_copies)
-    part_copies = dp_stage(part, 2)
+    arrive(part_copies.values())
+    part_copies = near_stage(part.at[pl.ds(zl * YH * ZH, YH * ZH)])
 
     own = jnp.zeros((images, emb_w), F32)
     for o in offsets:
@@ -187,17 +224,27 @@
         own = own + dot(pooled[kk], PW[kk])
 
     emb[pl.ds(slot, 1)] = own[None]
-    for stage in range(3):
-        arrive(dp_stage(emb, stage))
+    arrive(far_stage(emb))
+    y_copies = y_stage(emb)
+    copies = near_stage(row(emb, yh))
+    for j, copy in y_copies.items():
+        copy.wait_recv()
+        copies += near_stage(row(emb, lax.rem(yh - j + YH, YH)))
+    arrive(copies)
     arrive(part_copies)
 
     zall = emb[...].reshape(group, emb_w)
     center = jnp.mean(zall, axis=0, keepdims=True)
     zc = zall - center
     zbuf[...] = zc
-    square = zc * zc
-    spread = 2.0 * jnp.sum(square) / group
-    sq_row = dot(jnp.ones((8, emb_w), F32), square, ((1,), (1,)), HIGH)[0:1]
+    top = zc.astype(BF16)
+    parts[:, 0:emb_w] = top
+    parts[:, emb_w:] = (zc - top.astype(F32)).astype(BF16)
+    sq_col = jnp.sum(zc * zc, axis=1, keepdims=True)
+    spread = 2.0 * jnp.sum(sq_col) / group
+    sq_wide = jnp.broadcast_to(sq_col, (group, 128))
+    sqs[...] = sq_wide
+    sq_row = jnp.transpose(sq_wide)[0:1]
     lane = lax.broadcasted_iota(jnp.int32, (1, group), 1)
     ls = lane // images
     lzl = ls // (YH * ZH)
@@ -205,17 +252,17 @@
     lzh = ls % ZH
     member = (((lyh * ZH + lzh) * ZL + lzl) * images + lane % images).astype(F32)
 
-    step = 64 if group % 64 == 0 else group
+    step = 256 if group % 256 == 0 else group
     scale = 1.0 / (2.0 * spread)
 
     def kernel_rows(i, carry):
         col_sum, positive = carry
         rows = pl.ds(pl.multiple_of(i * (step // images), step // images), step // images)
         at = pl.ds(pl.multiple_of(i * step, step), step)
-        z = zbuf[at, :]
-        inner = dot(z, zbuf[...], ((1,), (1,)), HIGH)
-        sq = jnp.sum(z * z, axis=1, keepdims=True)
-        kk = jnp.exp(-(sq + sq_row - 2.0 * inner) * scale)
+        zt, zm = parts[at, 0:emb_w], parts[at, emb_w:]
+        inner = dot(jnp.concatenate([zt, zt], axis=1), parts[...], ((1,), (1,)))
+        inner = inner + dot(zm, parts[:, 0:emb_w], ((1,), (1,)))
+        kk = jnp.exp(-(sqs[at, 0:1] + sq_row - 2.0 * inner) * scale)
         kmat[at, :] = kk
         rcol[at, :] = jnp.broadcast_to(jnp.mean(kk, axis=1, keepdims=True), (step, 128))
         who = part[rows].reshape(step, 128)[:, 0:1]
@@ -247,9 +294,13 @@
     coeff = (-hot / group + 1.0 / (group * group) + GAMMA * cen / (scale_sq * root)) / (chips * 2)
     weighted = coeff * k_own
     z_own = zbuf[at, :]
+    w_top = weighted.astype(BF16)
+    w_low = (weighted - w_top.astype(F32)).astype(BF16)
+    moved = dot(w_top, parts[:, 0:emb_w]) + dot(w_top, parts[:, emb_w:])
+    moved = moved + dot(w_low, parts[:, 0:emb_w])
     grad = -(2.0 / spread) * (
         jnp.sum(weighted, axis=1, keepdims=True) * z_own
-        - dot(weighted, zbuf[...], precision=HIGH)
+        - moved
     )
     ge = grad.astype(BF16)
     geT = jnp.transpose(ge.astype(F32)).astype(BF16)
@@ -265,18 +316,28 @@
             term[n, half, 0:width] = conv_t[:, cols]
             term[n, half, width:] = proj_t[:, cols]
 
-    order = list(reversed(offsets))
+    order = [o for o in offsets if far(o)]
+    order += [o for o in offsets[1:] if o[0] == 0 and o[1] in (1, X - 1)]
+    order += [o for o in offsets[1:] if o not in order and o[0] == 0]
+    order += [o for o in offsets[1:] if o not in order] + [offsets[0]]
     core_copies = {}
+    relayed = {o: [] for o in offsets}
     group_copies = []
 
     def pair(n):
+        o = order[n]
         core_copies[n].wait_recv()
         total = term[n, pl.ds(c, 1)][0].astype(F32) + core_in[n].astype(F32)
+        for m, copy in relayed[o]:
+            copy.wait_recv()
+            total = total + group_in[m].astype(F32)
         pair_sum[n] = total.astype(BF16)
-        if n < len(order) - 1:
-            group_copies.append(
-                send(pair_sum.at[n], group_in.at[n], dev_chip(to_chip(order[n]), c))
-            )
+        if far(o):
+            copy = send(pair_sum.at[n], group_in.at[n], dev_chip(to_chip(second_hop(o)), c))
+            relayed[first_hop(o)].append((n, copy))
+        elif n < len(order) - 1:
+            copy = send(pair_sum.at[n], group_in.at[n], dev_chip(to_chip(o), c))
+            group_copies.append((n, copy))
 
     for n, o in enumerate(order):
         backward(n, to_chip(o))
@@ -285,20 +346,19 @@
             pair(n - 1)
     last = len(order) - 1
     pair(last)
-    arrive(group_copies)
     total = pair_sum[last].astype(F32)
-    for n in range(last):
+    for n, copy in group_copies:
+        copy.wait_recv()
         total = total + group_in[n].astype(F32)
     red0[...] = total.astype(BF16).reshape(red0.shape)
 
     copies = []
-    for j in range(1, ZL):
-        q = lax.rem(zl + j, ZL)
-        copies.append(send(red0.at[q], red0_in.at[j], dev_dp(yh, zh, q)))
+    for i, j in enumerate(near_z):
+        copies.append(send(red0.at[lax.rem(zl + j + ZL, ZL)], red0_in.at[i], dev_z(j)))
     arrive(copies)
     total = red0[zl].astype(F32)
-    for j in range(1, ZL):
-        total = total + red0_in[j].astype(F32)
+    for i in range(ZL - 1):
+        total = total + red0_in[i].astype(F32)
     red1[...] = total.astype(BF16)
     copies = []
     for j in range(1, ZH):
@@ -324,9 +384,8 @@
         copies.append(send(fin.at[zl, zh], fin.at[zl, zh], dev_dp(yh, q, zl)))
     arrive(copies)
     copies = []
-    for j in range(1, ZL):
-        q = lax.rem(zl + j, ZL)
-        copies.append(send(fin.at[zl], fin.at[zl], dev_dp(yh, zh, q)))
+    for j in near_z:
+        copies.append(send(fin.at[zl], fin.at[zl], dev_z(j)))
     arrive(copies)
 
     result = fin[...].astype(F32).reshape(width + emb_w, 128)
@@ -345,9 +404,8 @@
     group = dp * 8
     both = width + emb_w
     piece = both // (ZL * ZH)
-    sends = 2 * (chips - 1 + chips) + 2 * (YH + ZH + ZL - 3) + 2 * chips - 1
-    sends += 2 * (ZL - 1 + ZH - 1) + YH - 1
-    hbm = pl.BlockSpec(memory_space=pl.ANY)
+    sends = 100
+    hbm = pl.BlockSpec(memory_space=pltpu.HBM)
     vmem = pl.BlockSpec(memory_space=pltpu.VMEM)
     grad_conv, grad_proj, loss = pl.pallas_call(
         kernel,
@@ -369,6 +427,8 @@
             pltpu.VMEM((dp, 8, 128), F32),
             pltpu.VMEM((dp, 8, emb_w), F32),
             pltpu.VMEM((group, emb_w), F32),
+            pltpu.VMEM((group, 2 * emb_w), BF16),
+            pltpu.VMEM((group, 128), F32),
             pltpu.VMEM((group, group), F32),
             pltpu.VMEM((group, 128), F32),
             pltpu.VMEM((chips, 2, both, 128), BF16),
@@ -386,7 +446,7 @@
             pltpu.SemaphoreType.DMA((sends,)),
         ],
         compiler_params=pltpu.CompilerParams(
-            collective_id=0, has_side_effects=True, vmem_limit_bytes=48 << 20
+            collective_id=0, has_side_effects=True, vmem_limit_bytes=63 << 20
         ),
     )(features, shortcut, conv_weight, proj_weight, partner)
     return grad_conv, grad_proj, loss[0, 0:1]

time: 143 us -> 123 us (0.86); the launches traced: 140 us -> 122 us
  Pallas kernels: 132 us -> 117 us
  local copies, waits for them, and re-layouts: 6.17 us -> 3.24 us
    pallas_call x1, Pallas kernels: 132 us -> 117 us  [local(): pl.pallas_call(kernel, out_shape=(jax.ShapeDtypeStruct((128, width), F32)...]
    unnamed x12 -> x2, local copies, waits for them, and re-layouts: 6.17 us -> 3.24 us
where the time goes in v2:
time: 123 us; the launch traced here: 122 us
  Pallas kernels  117 us (95%)
  local copies, waits for them, and re-layouts  3.24 us (3%)
  between operations  2.39 us (2%)
    pallas_call x1, Pallas kernels, local(): pl.pallas_call(kernel, out_shape=(jax.ShapeDtypeStruct((128, width), F32)...  117 us
    unnamed x2, local copies, waits for them, and re-layouts  3.24 us

profile of v2, /device:TPU:6, one launch (start us, length us, event | category | flops | bytes accessed | tf_op | source)
XLA Modules:
  0.0 122.4 jit_solution(17084745652098385068)
XLA Ops:
  0.6 116.7 %shard_map.76 = (f32[128,512]{1,0:T(8,128)}, f32[128,256]{1,0:T(8,128)}, f32[1,128]{1,0:T(1,128)}) custom-call(bf16[392,512]{1,0:T(8,128)(2,1)} %feat_h.1, bf16[392,2048]{1,0:T(8,128)(2,1)} %short_h.1, bf16[128,512]{1,0:T(8,128)(2,1)} %conv_h.1, bf16[128,256]{1,0:T(8,128)(2,1)} %proj_h.1, s32[8]{0:T(128)} %partner_s.1), custom_call_target="tpu_custom_call" | custom-call | tf_op jit(solution)/shard_map/pallas_call | solution.py:410
  117.4 1.7 %copy.11 = f32[128,512]{1,0:T(8,128)} copy(f32[128,512]{1,0:T(8,128)} %get-tuple-element.12) | data formatting | bytes 524288
  119.0 1.6 %copy.12 = f32[128,256]{1,0:T(8,128)} copy(f32[128,256]{1,0:T(8,128)} %get-tuple-element.13) | data formatting | bytes 262144

commit v3 on v2

--- a/solution.py
+++ b/solution.py
@@ -29,6 +29,12 @@
     return (0, o[1]) if o[1] in (1, X - 1) else (o[0], 0)
 
 
+def z_plan(n):
+    if n == 16:
+        return [1, -1, 2, -2], 5, 13
+    return near(n), 0, 1
+
+
 def near(n):
     return [j if j <= n // 2 else j - n for j in sorted(range(1, n), key=lambda j: min(j, n - j))]
 
@@ -40,12 +46,12 @@
 
 
 def kernel(
-    feat_h, short_h, conv_h, proj_h, partner_s,
+    feat_h, short_h, conv_h, proj_h, partner_h,
     oconv, oproj, oloss,
     feat, short, featT, W, PW, hid, pooled, part, emb, zbuf, parts, sqs, kmat, rcol,
     term, core_in, pair_sum, group_in,
-    red0, red0_in, red1, red1_in, red2, fin,
-    lsem, ssem, rsem,
+    red0, close_in, red1, reach_in, opp_in, red2, done, close_done, opp_done, fin,
+    partner_s, lsem, ssem, rsem,
 ):
     chips = YL * X
     dp = YH * ZH * ZL
@@ -99,6 +105,7 @@
         pltpu.make_async_copy(feat_h, feat, lsem.at[1]),
         pltpu.make_async_copy(short_h, short, lsem.at[2]),
         pltpu.make_async_copy(proj_h, PW.at[chip, mine], lsem.at[3]),
+        pltpu.make_async_copy(partner_h, partner_s, lsem.at[4]),
     ]
     for copy in local:
         copy.start()
@@ -106,22 +113,27 @@
     peers = [dev_chip(chip, 1 - c)]
     peers += [dev_chip(to_chip(o), c) for o in offsets[1:] if not far(o)]
     peers += [dev_dp(lax.rem(yh + j, YH), zh, zl) for j in range(1, YH)]
-    peers += [dev_dp(yh, lax.rem(zh + j, ZH), zl) for j in range(1, ZH)]
+    Z = ZH * ZL
     z = zh * ZL + zl
 
+    def zmod(j):
+        return lax.rem(z + j + Z, Z)
+
     def dev_z(j):
-        q = lax.rem(z + j + ZH * ZL, ZH * ZL)
-        return (yh * ZH * ZL + q, f)
+        return (yh * Z + zmod(j), f)
 
     near_z = near(ZL)
-    for j in near_z:
-        peers.append(dev_z(j))
+    close, reach, inverse = z_plan(Z)
+    steps = near_z + close + [j * ZL for j in range(1, ZH)] + ([reach, 8] if reach else [])
+    steps = {j % Z for j in steps} | {-j % Z for j in steps}
+    peers += [dev_z(j) for j in sorted(steps)]
     barrier = pltpu.get_barrier_semaphore()
     for peer in peers:
         pl.semaphore_signal(barrier, inc=1, device_id=peer, device_id_type=MESH)
 
     slot = (zl * YH + yh) * ZH + zh
     row8 = lax.broadcasted_iota(jnp.int32, (images, 128), 0)
+    local[4].wait()
     column = jnp.zeros((images, 128), jnp.int32)
     for i in range(images):
         column = jnp.where(row8 == i, partner_s[i], column)
@@ -350,24 +362,38 @@
     for n, copy in group_copies:
         copy.wait_recv()
         total = total + group_in[n].astype(F32)
-    red0[...] = total.astype(BF16).reshape(red0.shape)
+    total = total.astype(BF16)
+    span = 3 if reach else 1
+    mid = span // 2
+    piece = red0.shape[1]
+    for p in range(Z + span - 1):
+        q = (reach * p) % Z if reach else p
+        red0[p] = total[q * piece : (q + 1) * piece]
+
+    def position(j):
+        return lax.rem(inverse * zmod(j) + Z - mid, Z)
 
     copies = []
-    for i, j in enumerate(near_z):
-        copies.append(send(red0.at[lax.rem(zl + j + ZL, ZL)], red0_in.at[i], dev_z(j)))
+    for i, j in enumerate(close):
+        copies.append(send(red0.at[pl.ds(position(j), span)], close_in.at[i], dev_z(j)))
+    if reach:
+        opposite = send(red0.at[lax.rem(inverse * zmod(8), Z)], opp_in, dev_z(8))
     arrive(copies)
-    total = red0[zl].astype(F32)
-    for i in range(ZL - 1):
-        total = total + red0_in[i].astype(F32)
-    red1[...] = total.astype(BF16)
-    copies = []
-    for j in range(1, ZH):
-        q = lax.rem(zh + j, ZH)
-        copies.append(send(red1.at[q], red1_in.at[j], dev_dp(yh, q, zl)))
-    arrive(copies)
-    total = red1[zh].astype(F32)
-    for j in range(1, ZH):
-        total = total + red1_in[j].astype(F32)
+    total = red0[pl.ds(position(0), span)].astype(F32)
+    for i in range(len(close)):
+        total = total + close_in[i].astype(F32)
+    if reach:
+        red1[...] = total.astype(BF16)
+        copies = [
+            send(red1.at[0], reach_in.at[0], dev_z(-reach)),
+            send(red1.at[2], reach_in.at[1], dev_z(reach)),
+        ]
+        opposite.wait_recv()
+        total = total[mid] + opp_in[...].astype(F32)
+        arrive(copies)
+        total = total + reach_in[0].astype(F32) + reach_in[1].astype(F32)
+    else:
+        total = total[mid]
     red2[yh] = total.astype(BF16)
     copies = []
     for j in range(1, YH):
@@ -377,16 +403,24 @@
     total = red2[0].astype(F32)
     for j in range(1, YH):
         total = total + red2[j].astype(F32)
-    fin[zl, zh] = total.astype(BF16)
-    copies = []
-    for j in range(1, ZH):
-        q = lax.rem(zh + j, ZH)
-        copies.append(send(fin.at[zl, zh], fin.at[zl, zh], dev_dp(yh, q, zl)))
-    arrive(copies)
-    copies = []
-    for j in near_z:
-        copies.append(send(fin.at[zl], fin.at[zl], dev_z(j)))
-    arrive(copies)
+    done[mid] = total.astype(BF16)
+    if reach:
+        copies = [
+            send(done.at[1], done.at[0], dev_z(reach)),
+            send(done.at[1], done.at[2], dev_z(-reach)),
+        ]
+        opposite = send(done.at[1], opp_done, dev_z(8))
+        arrive(copies)
+    copies = [send(done, close_done.at[i], dev_z(j)) for i, j in enumerate(close)]
+    for k in range(span):
+        fin[zmod(reach * (k - mid))] = done[k]
+    if reach:
+        opposite.wait_recv()
+        fin[zmod(8)] = opp_done[...]
+    for i, j in enumerate(close):
+        copies[i].wait_recv()
+        for k in range(span):
+            fin[zmod(reach * (k - mid) - j)] = close_done[i, k]
 
     result = fin[...].astype(F32).reshape(width + emb_w, 128)
     oconv[...] = jnp.transpose(result[0:width])
@@ -403,9 +437,14 @@
     dp = YH * ZH * ZL
     group = dp * 8
     both = width + emb_w
-    piece = both // (ZL * ZH)
+    Z = ZL * ZH
+    piece = both // Z
+    close, reach, _ = z_plan(Z)
+    span = 3 if reach else 1
     sends = 100
     hbm = pl.BlockSpec(memory_space=pltpu.HBM)
+    args = (features, shortcut, conv_weight, proj_weight, partner)
+    args = [pltpu.with_memory_space_constraint(arg, pltpu.HBM) for arg in args]
     vmem = pl.BlockSpec(memory_space=pltpu.VMEM)
     grad_conv, grad_proj, loss = pl.pallas_call(
         kernel,
@@ -414,7 +453,7 @@
             jax.ShapeDtypeStruct((128, emb_w), F32),
             jax.ShapeDtypeStruct((1, 128), F32),
         ),
-        in_specs=[hbm, hbm, hbm, hbm, pl.BlockSpec(memory_space=pltpu.SMEM)],
+        in_specs=[hbm] * 5,
         out_specs=(vmem, vmem, vmem),
         scratch_shapes=[
             pltpu.VMEM((rows, width), BF16),
@@ -435,20 +474,25 @@
             pltpu.VMEM((chips, both, 128), BF16),
             pltpu.VMEM((chips, both, 128), BF16),
             pltpu.VMEM((chips, both, 128), BF16),
-            pltpu.VMEM((ZL, ZH, piece, 128), BF16),
-            pltpu.VMEM((ZL, ZH, piece, 128), BF16),
-            pltpu.VMEM((ZH, piece, 128), BF16),
-            pltpu.VMEM((ZH, piece, 128), BF16),
+            pltpu.VMEM((Z + span - 1, piece, 128), BF16),
+            pltpu.VMEM((len(close) or 1, span, piece, 128), BF16),
+            pltpu.VMEM((span, piece, 128), BF16),
+            pltpu.VMEM((2, piece, 128), BF16),
+            pltpu.VMEM((piece, 128), BF16),
             pltpu.VMEM((YH, piece, 128), BF16),
-            pltpu.VMEM((ZL, ZH, piece, 128), BF16),
-            pltpu.SemaphoreType.DMA((4,)),
+            pltpu.VMEM((span, piece, 128), BF16),
+            pltpu.VMEM((len(close) or 1, span, piece, 128), BF16),
+            pltpu.VMEM((piece, 128), BF16),
+            pltpu.VMEM((Z, piece, 128), BF16),
+            pltpu.SMEM((8,), jnp.int32),
+            pltpu.SemaphoreType.DMA((5,)),
             pltpu.SemaphoreType.DMA((sends,)),
             pltpu.SemaphoreType.DMA((sends,)),
         ],
         compiler_params=pltpu.CompilerParams(
-            collective_id=0, has_side_effects=True, vmem_limit_bytes=63 << 20
+            collective_id=0, has_side_effects=True, vmem_limit_bytes=48 << 20
         ),
-    )(features, shortcut, conv_weight, proj_weight, partner)
+    )(*args)
     return grad_conv, grad_proj, loss[0, 0:1]
 
 

time: 123 us -> 116 us (0.943)
  Pallas kernels: 117 us -> 111 us
  local copies, waits for them, and re-layouts: 3.24 us -> 1.36 us
    pallas_call x1, Pallas kernels: 117 us -> 111 us  [local(): pl.pallas_call(kernel, out_shape=(jax.ShapeDtypeStruct((128, width), F32)...]
    unnamed x2, local copies, waits for them, and re-layouts: 3.24 us -> 1.36 us
where the time goes in v3:
time: 116 us; the launch traced here: 115 us
  Pallas kernels  111 us (96%)
  between operations  1.81 us (2%)
  local copies, waits for them, and re-layouts  1.36 us (1%)
    pallas_call x1, Pallas kernels, local(): pl.pallas_call(kernel, out_shape=(jax.ShapeDtypeStruct((128, width), F32)...  111 us

profile of v3, /device:TPU:6, one launch (start us, length us, event | category | flops | bytes accessed | tf_op | source)
XLA Modules:
  0.0 114.6 jit_solution(11061782186116671209)
XLA Ops:
  0.6 111.4 %shard_map.76 = (f32[128,512]{1,0:T(8,128)S(1)}, f32[128,256]{1,0:T(8,128)S(1)}, f32[1,128]{1,0:T(1,128)S(1)}) custom-call(bf16[392,512]{1,0:T(8,128)(2,1)} %feat_h.1, bf16[392,2048]{1,0:T(8,128)(2,1)} %short_h.1, bf16[128,512]{1,0:T(8,128)(2,1)} %conv_h.1, bf16[128,256]{1,0:T(8,128)(2,1)} %proj_h.1, s32[8]{0:T(128)} %partner_h.1), custom_call_target="tpu_custom_call" | custom-call | tf_op jit(solution)/shard_map/pallas_call | solution.py:449
  112.1 0.7 copy.11
  112.8 0.7 copy.12

commit v4 on v3

--- a/solution.py
+++ b/solution.py
@@ -89,6 +89,11 @@
         copy.start()
         pending.append(copy)
         return copy
+
+    def sent(n):
+        for copy in pending[:n]:
+            copy.wait_send()
+        del pending[:n]
 
     offsets = [(dy, dx) for dy in range(YL) for dx in range(X)]
     offsets.sort(key=lambda o: (far(o), o[0] + min(o[1], X - o[1]), -o[0]))
@@ -236,11 +241,22 @@
         own = own + dot(pooled[kk], PW[kk])
 
     emb[pl.ds(slot, 1)] = own[None]
-    arrive(far_stage(emb))
-    y_copies = y_stage(emb)
+    def to_y(zq):
+        view = emb.at[pl.ds((zl * YH + yh) * ZH + zq, 1)]
+        for j in near(YH):
+            y_copies[j].append(send(view, view, dev_dp(lax.rem(yh + j + YH, YH), zh, zl)))
+
+    y_copies = {j: [] for j in near(YH)}
+    older = len(pending)
+    far_copies = dict(zip(range(1, ZH), far_stage(emb)))
+    to_y(zh)
+    sent(older)
+    for j in near(ZH):
+        far_copies[j % ZH].wait_recv()
+        to_y(lax.rem(zh - j + ZH, ZH))
     copies = near_stage(row(emb, yh))
-    for j, copy in y_copies.items():
-        copy.wait_recv()
+    for j, landed_y in y_copies.items():
+        arrive(landed_y)
         copies += near_stage(row(emb, lax.rem(yh - j + YH, YH)))
     arrive(copies)
     arrive(part_copies)
@@ -330,7 +346,7 @@
 
     order = [o for o in offsets if far(o)]
     order += [o for o in offsets[1:] if o[0] == 0 and o[1] in (1, X - 1)]
-    order += [o for o in offsets[1:] if o not in order and o[0] == 0]
+    order += [o for o in offsets[1:] if o not in order and o[1] == 0]
     order += [o for o in offsets[1:] if o not in order] + [offsets[0]]
     core_copies = {}
     relayed = {o: [] for o in offsets}
@@ -374,10 +390,12 @@
         return lax.rem(inverse * zmod(j) + Z - mid, Z)
 
     copies = []
+    older = len(pending)
     for i, j in enumerate(close):
         copies.append(send(red0.at[pl.ds(position(j), span)], close_in.at[i], dev_z(j)))
     if reach:
         opposite = send(red0.at[lax.rem(inverse * zmod(8), Z)], opp_in, dev_z(8))
+    sent(older)
     arrive(copies)
     total = red0[pl.ds(position(0), span)].astype(F32)
     for i in range(len(close)):
@@ -396,9 +414,11 @@
         total = total[mid]
     red2[yh] = total.astype(BF16)
     copies = []
+    older = len(pending)
     for j in range(1, YH):
         q = lax.rem(yh + j, YH)
         copies.append(send(red2.at[yh], red2.at[yh], dev_dp(q, zh, zl)))
+    sent(older)
     arrive(copies)
     total = red2[0].astype(F32)
     for j in range(1, YH):
@@ -410,17 +430,25 @@
             send(done.at[1], done.at[2], dev_z(-reach)),
         ]
         opposite = send(done.at[1], opp_done, dev_z(8))
-        arrive(copies)
-    copies = [send(done, close_done.at[i], dev_z(j)) for i, j in enumerate(close)]
-    for k in range(span):
+    close_copies = []
+
+    def pass_on(k):
+        for i, j in enumerate(close):
+            copy = send(done.at[k], close_done.at[i, k], dev_z(j))
+            close_copies.append((i, j, k, copy))
         fin[zmod(reach * (k - mid))] = done[k]
+
+    pass_on(mid)
+    if reach:
+        for k, copy in zip((0, 2), copies):
+            copy.wait_recv()
+            pass_on(k)
     if reach:
         opposite.wait_recv()
         fin[zmod(8)] = opp_done[...]
-    for i, j in enumerate(close):
-        copies[i].wait_recv()
-        for k in range(span):
-            fin[zmod(reach * (k - mid) - j)] = close_done[i, k]
+    for i, j, k, copy in close_copies:
+        copy.wait_recv()
+        fin[zmod(reach * (k - mid) - j)] = close_done[i, k]
 
     result = fin[...].astype(F32).reshape(width + emb_w, 128)
     oconv[...] = jnp.transpose(result[0:width])
@@ -441,7 +469,7 @@
     piece = both // Z
     close, reach, _ = z_plan(Z)
     span = 3 if reach else 1
-    sends = 100
+    sends = 120
     hbm = pl.BlockSpec(memory_space=pltpu.HBM)
     args = (features, shortcut, conv_weight, proj_weight, partner)
     args = [pltpu.with_memory_space_constraint(arg, pltpu.HBM) for arg in args]

time: 116 us -> 115 us (level)
  no operation moved by 1% of the time
where the time goes in v4:
time: 115 us
  Pallas kernels  112 us (97%)
  between operations  1.81 us (2%)
  local copies, waits for them, and re-layouts  1.36 us (1%)
    pallas_call x1, Pallas kernels, local(): pl.pallas_call(kernel, out_shape=(jax.ShapeDtypeStruct((128, width), F32)...  112 us

profile of v4, /device:TPU:6, one launch (start us, length us, event | category | flops | bytes accessed | tf_op | source)
XLA Modules:
  0.0 114.7 jit_solution(10663017851551932674)
XLA Ops:
  0.6 111.5 %shard_map.76 = (f32[128,512]{1,0:T(8,128)S(1)}, f32[128,256]{1,0:T(8,128)S(1)}, f32[1,128]{1,0:T(1,128)S(1)}) custom-call(bf16[392,512]{1,0:T(8,128)(2,1)} %feat_h.1, bf16[392,2048]{1,0:T(8,128)(2,1)} %short_h.1, bf16[128,512]{1,0:T(8,128)(2,1)} %conv_h.1, bf16[128,256]{1,0:T(8,128)(2,1)} %proj_h.1, s32[8]{0:T(128)} %partner_h.1), custom_call_target="tpu_custom_call" | custom-call | tf_op jit(solution)/shard_map/pallas_call | solution.py:477
  112.1 0.7 copy.11
  112.9 0.7 copy.12

commit v5 on v4

--- a/solution.py
+++ b/solution.py
@@ -104,6 +104,27 @@
     def from_chip(o):
         return lax.rem(yl + YL - o[0], YL) * X + lax.rem(x + X - o[1], X)
 
+    peers = [dev_chip(chip, 1 - c)]
+    peers += [dev_chip(to_chip(o), c) for o in offsets[1:] if not far(o)]
+    peers += [dev_dp(lax.rem(yh + j, YH), zh, zl) for j in range(1, YH)]
+    Z = ZH * ZL
+    z = zh * ZL + zl
+
+    def zmod(j):
+        return lax.rem(z + j + Z, Z)
+
+    def dev_z(j):
+        return (yh * Z + zmod(j), f)
+
+    near_z = near(ZL)
+    close, reach, inverse = z_plan(Z)
+    steps = near_z + close + [j * ZL for j in range(1, ZH)] + ([reach, 8] if reach else [])
+    steps = {j % Z for j in steps} | {-j % Z for j in steps}
+    peers += [dev_z(j) for j in sorted(steps, key=lambda j: min(j, Z - j))]
+    barrier = pltpu.get_barrier_semaphore()
+    for peer in reversed(peers):
+        pl.semaphore_signal(barrier, inc=1, device_id=peer, device_id_type=MESH)
+
     mine = pl.ds(pl.multiple_of(c * 128, 128), 128)
     local = [
         pltpu.make_async_copy(conv_h, W.at[chip, mine], lsem.at[0]),
@@ -114,27 +135,6 @@
     ]
     for copy in local:
         copy.start()
-
-    peers = [dev_chip(chip, 1 - c)]
-    peers += [dev_chip(to_chip(o), c) for o in offsets[1:] if not far(o)]
-    peers += [dev_dp(lax.rem(yh + j, YH), zh, zl) for j in range(1, YH)]
-    Z = ZH * ZL
-    z = zh * ZL + zl
-
-    def zmod(j):
-        return lax.rem(z + j + Z, Z)
-
-    def dev_z(j):
-        return (yh * Z + zmod(j), f)
-
-    near_z = near(ZL)
-    close, reach, inverse = z_plan(Z)
-    steps = near_z + close + [j * ZL for j in range(1, ZH)] + ([reach, 8] if reach else [])
-    steps = {j % Z for j in steps} | {-j % Z for j in steps}
-    peers += [dev_z(j) for j in sorted(steps)]
-    barrier = pltpu.get_barrier_semaphore()
-    for peer in peers:
-        pl.semaphore_signal(barrier, inc=1, device_id=peer, device_id_type=MESH)
 
     slot = (zl * YH + yh) * ZH + zh
     row8 = lax.broadcasted_iota(jnp.int32, (images, 128), 0)

time: 115 us -> 114 us (level)
  no operation moved by 1% of the time
where the time goes in v5:
time: 114 us
  Pallas kernels  111 us (97%)
  between operations  1.81 us (2%)
  local copies, waits for them, and re-layouts  1.36 us (1%)
    pallas_call x1, Pallas kernels, local(): pl.pallas_call(kernel, out_shape=(jax.ShapeDtypeStruct((128, width), F32)...  111 us

profile of v5, /device:TPU:6, one launch (start us, length us, event | category | flops | bytes accessed | tf_op | source)
XLA Modules:
  0.0 114.1 jit_solution(2481029000910377722)
XLA Ops:
  0.6 110.9 %shard_map.76 = (f32[128,512]{1,0:T(8,128)S(1)}, f32[128,256]{1,0:T(8,128)S(1)}, f32[1,128]{1,0:T(1,128)S(1)}) custom-call(bf16[392,512]{1,0:T(8,128)(2,1)} %feat_h.1, bf16[392,2048]{1,0:T(8,128)(2,1)} %short_h.1, bf16[128,512]{1,0:T(8,128)(2,1)} %conv_h.1, bf16[128,256]{1,0:T(8,128)(2,1)} %proj_h.1, s32[8]{0:T(128)} %partner_h.1), custom_call_target="tpu_custom_call" | custom-call | tf_op jit(solution)/shard_map/pallas_call | solution.py:477
  111.6 0.7 copy.11
  112.3 0.7 copy.12
